TPU v7x, 128 devices: a whole 4x4x4 slice. The times are simulated.
128 devices in a mesh: leaf: 2 (over core), front: 64 (over z, y, x).
Axes of the slice: x: 4, y: 4, z: 4, core: 2. Of those that a mesh axis runs over, the one named last changes fastest.
Arguments:
- front_block: float32 [8192, 8192], P('leaf', 'front'), as said below
- child_update: float32 [2, 6144, 8192], P('leaf', None, 'front'), as said below
- child_map: int32 [2, 48], P('leaf'), may hold values from 0 to 63, as said below
Outputs:
- factored: float32 [8192, 8192], P('leaf', 'front')
Inputs may be any that keep to these rules, and one draw needn't show every extreme that they name: `child_map`: each row is strictly increasing, holds 48 distinct blocks, and always names block 0 and block 63. `front_block`: Symmetric; the assembled front is positive definite. `child_update`: each child's update is symmetric and positive semidefinite in the child's order; columns of parent blocks that the child's map does not name are zero.
All inputs are finite; a program needn't handle non-finite values.
Results may differ from a plain program's by a relative error of at most 0.000088.
Values sent between devices are 32-bit elements; how exact they have to be, the bound alone decides.
A program may use at most 128 MiB of HBM per device.

v0:
```python
import jax
import jax.numpy as jnp
from jax import lax
from jax.sharding import PartitionSpec as P

BLK = 128
S = 512
HIGHEST = lax.Precision.HIGHEST


def gather_half(blocks, child_map, half, half_blocks):
    parent = half * half_blocks + jnp.arange(half_blocks, dtype=jnp.int32)
    hit = child_map[None, :] == parent[:, None]
    found = jnp.any(hit, axis=1)
    index = jnp.argmax(hit, axis=1)
    picked = jnp.take(blocks, index, axis=0)
    picked = jnp.where(found[:, None, None], picked, jnp.zeros_like(picked))
    return picked.reshape(half_blocks * BLK, blocks.shape[2])


def per_device(front_block, child_update, child_map):
    rows, cols = front_block.shape
    n_leaf = lax.axis_size("leaf")
    n_front = lax.axis_size("front")
    leaf = lax.axis_index("leaf")
    front = lax.axis_index("front")
    half_blocks = rows // BLK
    blocks = child_update[0].reshape(-1, BLK, cols)
    cmap = child_map[0]
    own = gather_half(blocks, cmap, leaf, half_blocks)
    send = gather_half(blocks, cmap, 1 - leaf, half_blocks)
    recv = lax.ppermute(send, "leaf", [(0, 1), (1, 0)])
    first = jnp.where(leaf == 0, own, recv)
    second = jnp.where(leaf == 0, recv, own)
    assembled = front_block + first + second
    top = assembled[:S]
    piv_cols = S // cols
    is_piv = front < piv_cols
    col_at = jnp.minimum(front, piv_cols - 1) * cols
    panel = lax.dynamic_update_slice_in_dim(
        jnp.zeros((S, S), jnp.float32), jnp.where(is_piv, top, jnp.zeros_like(top)), col_at, 1
    )
    pivot = lax.psum(panel, "front")
    factor = jnp.linalg.cholesky(pivot)
    own_solved = lax.linalg.triangular_solve(factor, top, left_side=True, lower=True).T
    from_leaf0 = lax.ppermute(own_solved, "leaf", [(0, 1)])
    col_solved = jnp.where(leaf == 0, own_solved, from_leaf0)
    piece = rows // n_front
    per_block = BLK // piece
    pieces = []
    for part in range(per_block):
        pairs = []
        for lf in range(n_leaf):
            for k in range(n_front // per_block):
                src = lf * n_front + lf * half_blocks + k
                dst = lf * n_front + per_block * k + part
                pairs.append((src, dst))
        pieces.append(
            lax.ppermute(col_solved[part * piece : (part + 1) * piece], ("leaf", "front"), pairs)
        )
    my_piece = pieces[0]
    for part in range(1, per_block):
        my_piece = jnp.where(front % per_block == part, pieces[part], my_piece)
    row_solved = lax.all_gather(my_piece, "front", tiled=True)
    schur = assembled - jnp.dot(row_solved, col_solved.T, precision=HIGHEST)
    row_global = leaf * rows + jnp.arange(rows, dtype=jnp.int32)
    col_global = front * cols + jnp.arange(cols, dtype=jnp.int32)
    col_start = jnp.minimum(front * cols, S - cols)
    left_rows = lax.dynamic_slice_in_dim(row_solved, col_start, cols, 1)
    left_top = jnp.pad(
        lax.dynamic_slice_in_dim(factor, col_start, cols, 1), ((0, rows - S), (0, 0))
    )
    left_part = jnp.where(row_global[:, None] < S, left_top, left_rows)
    right_top = jnp.pad(col_solved.T, ((0, rows - S), (0, 0)))
    right_part = jnp.where(row_global[:, None] < S, right_top, schur)
    return jnp.where(col_global[None, :] < S, left_part, right_part)


def solution(mesh):
    return jax.shard_map(
        per_device,
        mesh=mesh,
        in_specs=(P("leaf", "front"), P("leaf", None, "front"), P("leaf", None)),
        out_specs=P("leaf", "front"),
        check_vma=False,
    )
```

profile of v0, /device:TPU:1, one launch (start us, length us, event | category | flops | bytes accessed | tf_op | source)
XLA Modules:
  0.0 471.3 jit_solution(12014427817205239228)
XLA Ops:
  6.5 1.5 compare_reduce_fusion
  8.9 1.4 compare_reduce_fusion.2
  10.3 2.0 gather_fusion.1
  12.3 3.2 select_select_fusion
  15.5 2.9 copy.84
  18.4 1.4 collective-permute-start
  19.9 2.0 gather_fusion
  21.8 3.2 select_select_fusion.1
  25.1 2.9 copy.83
  28.0 2.9 copy.56
  30.8 3.3 select_add_fusion
  34.1 1.4 broadcast_in_dim.58
  37.1 129.3 %all-reduce.5.cloned.1.call-done = f32[512,512]{0,1:T(8,128)} async-done(((f32[512,512]{0,1:T(8,128)}), f32[512,512]{0,1:T(8,128)}) %all-reduce.5.cloned.1.call-update) | async-done | bytes 1048592 | tf_op jit(solution)/shard_map/psum | solution.py:43
  166.4 2.6 copy.57
  169.0 1.8 fusion
  171.8 11.7 %cholesky.103 = f32[128,128]{1,0:T(8,128)S(1)} custom-call(f32[128,128]{1,0:T(8,128)S(1)} %cholesky.263), custom_call_target="Cholesky" | custom-call | tf_op jit(solution)/shard_map/jit(cholesky)/cholesky | solution.py:44
  184.3 9.8 %custom-call.30 = f32[1,128,128]{1,2,0:T(8,128)S(1)} custom-call(f32[1,128,128]{2,1,0:T(8,128)S(1)} %get-tuple-element.55), custom_call_target="InvertDiagBlocksLowerTriangular" | custom-call | tf_op jit(solution)/shard_map/jit(cholesky)/cholesky | solution.py:44
  195.3 1.9 convolution_subtract_fusion.1
  197.4 1.5 cholesky.267
  198.9 13.2 %cholesky.215 = f32[128,128]{1,0:T(8,128)} custom-call(f32[128,128]{1,0:T(8,128)} %cholesky.267), custom_call_target="Cholesky" | custom-call | tf_op jit(solution)/shard_map/jit(cholesky)/cholesky | solution.py:44
  212.1 1.5 copy.60
  213.6 1.5 select_reduce_fusion.2
  215.1 11.4 %custom-call.31 = f32[1,128,128]{1,2,0:T(8,128)} custom-call(f32[1,128,128]{2,1,0:T(8,128)} %get-tuple-element.53), custom_call_target="InvertDiagBlocksLowerTriangular" | custom-call | tf_op jit(solution)/shard_map/jit(cholesky)/cholesky | solution.py:44
  230.6 1.5 convolution_subtract_fusion.2
  232.1 11.7 %cholesky.236 = f32[128,128]{1,0:T(8,128)S(1)} custom-call(f32[128,128]{1,0:T(8,128)S(1)} %cholesky.272), custom_call_target="Cholesky" | custom-call | tf_op jit(solution)/shard_map/jit(cholesky)/cholesky | solution.py:44
  244.6 9.8 %custom-call.32 = f32[1,128,128]{1,2,0:T(8,128)S(1)} custom-call(f32[1,128,128]{2,1,0:T(8,128)S(1)} %get-tuple-element.51), custom_call_target="InvertDiagBlocksLowerTriangular" | custom-call | tf_op jit(solution)/shard_map/jit(cholesky)/cholesky | solution.py:44
  255.3 1.5 convolution_subtract_fusion.3
  256.8 11.9 %cholesky.253 = f32[128,128]{1,0:T(8,128)S(1)} custom-call(f32[128,128]{1,0:T(8,128)S(1)} %convolution_subtract_fusion.3), custom_call_target="Cholesky" | custom-call | tf_op jit(solution)/shard_map/jit(cholesky)/cholesky | solution.py:44
  274.7 1.6 fusion.1
  276.3 14.5 %while.1 = (s32[]{:T(128)}, f32[512,512]{0,1:T(8,128)}, s32[4,2]{0,1:T(2,128)S(1)}, f32[4,128,128]{2,1,0:T(8,128)}, s32[]{:T(128)}) while((s32[]{:T(128)}, f32[512,512]{0,1:T(8,128)}, s32[4,2]{0,1:T(2,128)S(1)}, f32[4,128,128]{2,1,0:T(8,128)}, s32[]{:T(128)}) %tuple.35), condition=%wide.while_cond, body=%wide.while_body.sunk | while | flops 2 | bytes 393329 | solution.py:45
  277.0 2.2 dynamic-slice.7
  280.6 2.2 dynamic-slice.7
  284.3 2.2 dynamic-slice.7
  287.9 2.2 dynamic-slice.7
  290.8 40.1 %custom-call.33 = f32[4,128,128]{1,2,0:T(8,128)S(1)} custom-call(f32[4,128,128]{2,1,0:T(8,128)} %get-tuple-element.17), custom_call_target="InvertDiagBlocksLowerTriangular" | custom-call | tf_op jit(solution)/shard_map/triangular_solve | solution.py:45
  335.3 1.3 fusion.14
  337.8 2.0 fusion.4
  341.1 1.3 collective-permute-start.1
  342.4 4.9 %collective-permute-done.1 = f32[128,512]{1,0:T(8,128)S(1)} collective-permute-done((f32[128,512]{1,0:T(8,128)S(1)}, f32[128,512]{1,0:T(8,128)S(1)}, u32[]{:S(2)}, u32[]{:S(2)}) %collective-permute-start.1) | collective-permute-done | bytes 262176 | tf_op jit(solution)/shard_map/ppermute | solution.py:46
  348.8 1.3 collective-permute-start.3
  350.1 1.3 collective-permute-start.2
  351.4 4.8 %collective-permute-done.3 = f32[64,512]{1,0:T(8,128)S(1)} collective-permute-done((f32[64,512]{1,0:T(8,128)}, f32[64,512]{1,0:T(8,128)S(1)}, u32[]{:S(2)}, u32[]{:S(2)}) %collective-permute-start.3) | collective-permute-done | bytes 131104 | tf_op jit(solution)/shard_map/ppermute | solution.py:59
  357.0 1.7 constant_dynamic-slice_fusion.2
  358.7 80.8 %all-gather.2.cloned.1.call-done = f32[4096,512]{1,0:T(8,128)} async-done(((f32[64,512]{1,0:T(8,128)}), f32[4096,512]{1,0:T(8,128)}) %all-gather.2.cloned.1.call-update) | async-done | bytes 8388624 | tf_op jit(solution)/shard_map/all_gather | solution.py:64
  439.5 4.2 constant_dynamic-slice_fusion.1
  443.7 2.9 copy.86
  446.6 14.8 %select_select_fusion.2 = f32[4096,128]{0,1:T(8,128)} fusion(f32[512,128]{0,1:T(8,128)S(1)} %bitcast.58, f32[4096,128]{0,1:T(8,128)} %copy.86, f32[512,128]{0,1:T(8,128)} %constant_dynamic-slice_fusion.2, pred[128]{0:T(512)(128)(4,1)S(1)} %add_compare_fusion.1, pred[4096]{0:T(1024)(128)(4,1)S(1)} %add_compare_fusion, f32[4096,128]{0,1:T(8,128)} %copy-done.1, ...), kind=kOutput, calls=%fused_computation.7 | convolution fusion | flops 3223322624 | bytes 15470720 | tf_op jit(solution)/shard_map/dot_general | solution.py:65
  461.4 2.9 copy.75
  (82 shorter events, 29.3 us)
Async XLA Ops:
  6.5 3.8 copy-start
  6.5 159.9 %all-reduce.5.cloned.1.call-start = ((), (), s32[]{:S(2)}) async-start(), calls=%async_computation | async-start | bytes 2097152 | tf_op jit(solution)/shard_map/psum | solution.py:43
  18.4 12.4 %collective-permute-start = (f32[4096,128]{0,1:T(8,128)}, f32[4096,128]{0,1:T(8,128)}, u32[]{:S(2)}, u32[]{:S(2)}) collective-permute-start(f32[4096,128]{0,1:T(8,128)} %copy.84), channel_id=1, source_target_pairs={{0,64},{64,0},{1,65},{65,1},{2,66},{66,2},{3,67},{67,3},{4,68},{68... | collective-permute-start | bytes 6291464 | tf_op jit(solution)/shard_map/ppermute | solution.py:32
  34.1 1.7 copy-start.1
  36.6 403.0 %all-gather.2.cloned.1.call-start = ((), (), s32[]{:S(2)}) async-start(), calls=%async_computation.1 | async-start | bytes 8519680 | tf_op jit(solution)/shard_map/all_gather | solution.py:64
  170.8 1.0 copy-start.3
  197.4 31.0 %copy-start.4 = (f32[384,128]{1,0:T(8,128)S(1)}, f32[384,128]{1,0:T(8,128)}, u32[]{:S(2)}) copy-start(f32[384,128]{1,0:T(8,128)} %convolution_subtract_fusion.1) | copy-start | bytes 589828
  229.5 1.0 copy-start.2
  331.0 0.7 copy-start.6
  339.9 2.5 copy-start.5
  341.1 6.2 %collective-permute-start.1 = (f32[128,512]{1,0:T(8,128)S(1)}, f32[128,512]{1,0:T(8,128)S(1)}, u32[]{:S(2)}, u32[]{:S(2)}) collective-permute-start(f32[128,512]{1,0:T(8,128)S(1)} %maximum_bitcast_fusion), channel_id=1, source_target_pairs={{0,64},{1,65},{2,66},{3,67},{4,68},{5,69},{6,70},{7,71},{8,72},{9,... | collective-permute-start | bytes 786440 | tf_op jit(solution)/shard_map/ppermute | solution.py:46
  348.8 7.4 %collective-permute-start.3 = (f32[64,512]{1,0:T(8,128)}, f32[64,512]{1,0:T(8,128)S(1)}, u32[]{:S(2)}, u32[]{:S(2)}) collective-permute-start(f32[64,512]{1,0:T(8,128)} %get-tuple-element.48), channel_id=1, source_target_pairs={{0,0},{1,2},{2,4},{3,6},{4,8},{5,10},{6,12},{7,14},{8,16},{9,18},{... | collective-permute-start | bytes 393224 | tf_op jit(solution)/shard_map/ppermute | solution.py:59
  350.1 6.1 %collective-permute-start.2 = (f32[64,512]{1,0:T(8,128)}, f32[64,512]{1,0:T(8,128)}, u32[]{:S(2)}, u32[]{:S(2)}) collective-permute-start(f32[64,512]{1,0:T(8,128)} %get-tuple-element.49), channel_id=1, source_target_pairs={{0,1},{1,3},{2,5},{3,7},{4,9},{5,11},{6,13},{7,15},{8,17},{9,19},{... | collective-permute-start | bytes 393224 | tf_op jit(solution)/shard_map/ppermute | solution.py:59
Sparse Core Ops, SparseCore 0:
  36.7 129.7 all-reduce.4
  357.1 82.4 all-gather.1
where the time goes:
time: 476 us; the launch traced here: 471 us
  waiting for transfers between devices  220 us (46%)
  other arithmetic  143 us (30%)
  local copies, waits for them, and re-layouts  54 us (11%)
  matrix products  32.1 us (7%)
  between operations  16.5 us (3%)
  starting transfers between devices  5.81 us (1%)
    psum x1, waiting for transfers between devices, per_device(): pivot = lax.psum(panel, 'front')  129 us
    another operation x15, other arithmetic, per_device(): factor = jnp.linalg.cholesky(pivot)  83.8 us
    all_gather x1, waiting for transfers between devices, per_device(): row_solved = lax.all_gather(my_piece, 'front', tiled=True)  80.8 us
    another operation x3, other arithmetic, per_device(): lax.linalg.triangular_solve(factor, top, left_side=True, lower=True)  41.7 us
    dot_general x1, matrix products, per_device(): schur = assembled - jnp.dot(row_solved, col_solved.T, precision=HIGHEST)  14.8 us
    another operation x20, local copies, waits for them, and re-layouts  14.5 us
  transfers between devices with their start and end apart: 6, of which 4 were waited for; matrix products, arithmetic and copies ran while one was open for 3% of the time, Pallas kernels for 0%

commit v1 on v0

--- a/solution.py
+++ b/solution.py
@@ -61,7 +61,9 @@
     my_piece = pieces[0]
     for part in range(1, per_block):
         my_piece = jnp.where(front % per_block == part, pieces[part], my_piece)
-    row_solved = lax.all_gather(my_piece, "front", tiled=True)
+    row_solved = jnp.concatenate(
+        lax.all_to_all(jnp.stack([my_piece] * lax.axis_size("front")), "front", 0, 0), axis=0
+    )
     schur = assembled - jnp.dot(row_solved, col_solved.T, precision=HIGHEST)
     row_global = leaf * rows + jnp.arange(rows, dtype=jnp.int32)
     col_global = front * cols + jnp.arange(cols, dtype=jnp.int32)

time: 476 us -> 525 us (1.10)
  the two profiles are of different devices: /device:TPU:1 before, /device:TPU:4 now
where the time goes in v1:
time: 525 us; the launch traced here: 521 us
  waiting for transfers between devices  248 us (47%)
  other arithmetic  144 us (27%)
  local copies, waits for them, and re-layouts  58.6 us (11%)
  matrix products  32.1 us (6%)
  starting transfers between devices  22 us (4%)
  between operations  16.5 us (3%)
    psum x1, waiting for transfers between devices, per_device(): pivot = lax.psum(panel, 'front')  131 us
    all_to_all x1, waiting for transfers between devices, per_device(): lax.all_to_all(jnp.stack([my_piece] * lax.axis_size('front')), 'front', 0...  114 us
    another operation x15, other arithmetic, per_device(): factor = jnp.linalg.cholesky(pivot)  84.1 us
    another operation x3, other arithmetic, per_device(): lax.linalg.triangular_solve(factor, top, left_side=True, lower=True)  43 us
    dot_general x1, matrix products, per_device(): schur = assembled - jnp.dot(row_solved, col_solved.T, precision=HIGHEST)  14.8 us
    another operation x20, local copies, waits for them, and re-layouts  14.5 us
    all_to_all x1, starting transfers between devices, per_device(): lax.all_to_all(jnp.stack([my_piece] * lax.axis_size('front')), 'front', 0...  13.6 us
  transfers between devices with their start and end apart: 6, of which 4 were waited for; matrix products, arithmetic and copies ran while one was open for 2% of the time, Pallas kernels for 0%

profile of v1, /device:TPU:4, one launch (start us, length us, event | category | flops | bytes accessed | tf_op | source)
XLA Modules:
  0.0 521.3 jit_solution(1699008181446185633)
XLA Ops:
  6.5 1.5 compare_reduce_fusion
  8.9 1.4 compare_reduce_fusion.2
  10.3 2.0 gather_fusion.1
  12.3 3.2 select_select_fusion
  15.5 2.9 copy.70
  18.4 2.0 gather_fusion
  20.4 3.2 select_select_fusion.1
  23.6 2.9 copy.69
  26.5 3.1 copy.42
  29.7 3.3 select_add_fusion
  33.0 1.3 broadcast_in_dim.58
  35.4 130.9 %all-reduce.5.cloned.1.call-done = f32[512,512]{0,1:T(8,128)} async-done(((f32[512,512]{0,1:T(8,128)}), f32[512,512]{0,1:T(8,128)}) %all-reduce.5.cloned.1.call-update) | async-done | bytes 1048592 | tf_op jit(solution)/shard_map/psum | solution.py:43
  166.3 2.6 copy.43
  168.9 1.8 fusion
  171.6 11.7 %cholesky.103 = f32[128,128]{1,0:T(8,128)S(1)} custom-call(f32[128,128]{1,0:T(8,128)S(1)} %cholesky.263), custom_call_target="Cholesky" | custom-call | tf_op jit(solution)/shard_map/jit(cholesky)/cholesky | solution.py:44
  184.1 9.8 %custom-call.30 = f32[1,128,128]{1,2,0:T(8,128)S(1)} custom-call(f32[1,128,128]{2,1,0:T(8,128)S(1)} %get-tuple-element.51), custom_call_target="InvertDiagBlocksLowerTriangular" | custom-call | tf_op jit(solution)/shard_map/jit(cholesky)/cholesky | solution.py:44
  195.2 1.9 convolution_subtract_fusion.1
  197.2 1.5 cholesky.267
  198.8 13.2 %cholesky.215 = f32[128,128]{1,0:T(8,128)} custom-call(f32[128,128]{1,0:T(8,128)} %cholesky.267), custom_call_target="Cholesky" | custom-call | tf_op jit(solution)/shard_map/jit(cholesky)/cholesky | solution.py:44
  211.9 1.5 copy.46
  213.5 1.5 select_reduce_fusion.2
  215.0 11.8 %custom-call.31 = f32[1,128,128]{1,2,0:T(8,128)} custom-call(f32[1,128,128]{2,1,0:T(8,128)} %get-tuple-element.49), custom_call_target="InvertDiagBlocksLowerTriangular" | custom-call | tf_op jit(solution)/shard_map/jit(cholesky)/cholesky | solution.py:44
  230.8 1.5 convolution_subtract_fusion.2
  232.3 11.7 %cholesky.236 = f32[128,128]{1,0:T(8,128)S(1)} custom-call(f32[128,128]{1,0:T(8,128)S(1)} %cholesky.272), custom_call_target="Cholesky" | custom-call | tf_op jit(solution)/shard_map/jit(cholesky)/cholesky | solution.py:44
  244.8 9.8 %custom-call.32 = f32[1,128,128]{1,2,0:T(8,128)S(1)} custom-call(f32[1,128,128]{2,1,0:T(8,128)S(1)} %get-tuple-element.47), custom_call_target="InvertDiagBlocksLowerTriangular" | custom-call | tf_op jit(solution)/shard_map/jit(cholesky)/cholesky | solution.py:44
  255.5 1.5 convolution_subtract_fusion.3
  257.0 11.9 %cholesky.253 = f32[128,128]{1,0:T(8,128)S(1)} custom-call(f32[128,128]{1,0:T(8,128)S(1)} %convolution_subtract_fusion.3), custom_call_target="Cholesky" | custom-call | tf_op jit(solution)/shard_map/jit(cholesky)/cholesky | solution.py:44
  274.9 2.9 fusion.1
  277.8 14.5 %while.1 = (s32[]{:T(128)}, f32[512,512]{0,1:T(8,128)}, s32[4,2]{0,1:T(2,128)S(1)}, f32[4,128,128]{2,1,0:T(8,128)}, s32[]{:T(128)}) while((s32[]{:T(128)}, f32[512,512]{0,1:T(8,128)}, s32[4,2]{0,1:T(2,128)S(1)}, f32[4,128,128]{2,1,0:T(8,128)}, s32[]{:T(128)}) %tuple.34), condition=%wide.while_cond, body=%wide.while_body.sunk | while | flops 2 | bytes 393329 | solution.py:45
  278.5 2.2 dynamic-slice.7
  282.1 2.2 dynamic-slice.7
  285.8 2.2 dynamic-slice.7
  289.4 2.2 dynamic-slice.7
  292.3 40.1 %custom-call.33 = f32[4,128,128]{1,2,0:T(8,128)S(1)} custom-call(f32[4,128,128]{2,1,0:T(8,128)} %get-tuple-element.17), custom_call_target="InvertDiagBlocksLowerTriangular" | custom-call | tf_op jit(solution)/shard_map/triangular_solve | solution.py:45
  336.8 1.3 fusion.14
  339.3 2.0 fusion.4
  342.6 1.3 collective-permute-start.1
  346.6 3.6 collective-permute-start.3
  350.2 3.5 collective-permute-start.2
  353.7 2.2 collective-permute-done.2
  355.9 4.3 stack.2
  360.2 13.6 %all-to-all-start = ((f32[64,64,512]{2,1,0:T(8,128)}), f32[64,64,512]{2,1,0:T(8,128)}, u32[]{:S(2)}, u32[]{:S(2)}) async-start(f32[64,64,512]{2,1,0:T(8,128)} %stack.2), calls=%async_computation | async-start | bytes 16777216 | tf_op jit(solution)/shard_map/all_to_all | solution.py:65
  373.9 1.7 constant_dynamic-slice_fusion.2
  375.6 113.9 %all-to-all-done = f32[64,64,512]{2,1,0:T(8,128)} async-done(((f32[64,64,512]{2,1,0:T(8,128)}), f32[64,64,512]{2,1,0:T(8,128)}, u32[]{:S(2)}, u32[]{:S(2)}) %all-to-all-start) | async-done | bytes 8388640 | tf_op jit(solution)/shard_map/all_to_all | solution.py:65
  489.5 4.2 constant_dynamic-slice_fusion.1
  493.7 2.9 copy.72
  496.6 14.8 %select_select_fusion.2 = f32[4096,128]{0,1:T(8,128)} fusion(f32[512,128]{0,1:T(8,128)S(1)} %bitcast.59, f32[4096,128]{0,1:T(8,128)} %copy.72, f32[512,128]{0,1:T(8,128)} %constant_dynamic-slice_fusion.2, pred[128]{0:T(512)(128)(4,1)S(1)} %add_compare_fusion.1, pred[4096]{0:T(1024)(128)(4,1)S(1)} %add_compare_fusion, f32[4096,128]{0,1:T(8,128)} %copy-done.1, ...), kind=kOutput, calls=%fused_computation.7 | convolution fusion | flops 3223322624 | bytes 15470720 | tf_op jit(solution)/shard_map/dot_general | solution.py:67
  511.4 2.9 copy.61
  (82 shorter events, 29.3 us)
Async XLA Ops:
  6.5 3.8 copy-start
  6.5 159.7 %all-reduce.5.cloned.1.call-start = ((), (), s32[]{:S(2)}) async-start(), calls=%async_computation.1 | async-start | bytes 2097152 | tf_op jit(solution)/shard_map/psum | solution.py:43
  18.4 11.3 %collective-permute-start = (f32[4096,128]{0,1:T(8,128)}, f32[4096,128]{0,1:T(8,128)}, u32[]{:S(2)}, u32[]{:S(2)}) collective-permute-start(f32[4096,128]{0,1:T(8,128)} %copy.70), channel_id=1, source_target_pairs={{0,64},{64,0},{1,65},{65,1},{2,66},{66,2},{3,67},{67,3},{4,68},{68... | collective-permute-start | bytes 6291464 | tf_op jit(solution)/shard_map/ppermute | solution.py:32
  33.0 1.7 copy-start.1
  170.6 1.0 copy-start.3
  197.2 31.3 %copy-start.4 = (f32[384,128]{1,0:T(8,128)S(1)}, f32[384,128]{1,0:T(8,128)}, u32[]{:S(2)}) copy-start(f32[384,128]{1,0:T(8,128)} %convolution_subtract_fusion.1) | copy-start | bytes 589828
  229.7 1.0 copy-start.2
  332.5 0.7 copy-start.6
  341.4 2.5 copy-start.5
  342.6 2.4 collective-permute-start.1
  346.6 7.1 %collective-permute-start.3 = (f32[64,512]{1,0:T(8,128)}, f32[64,512]{1,0:T(8,128)S(1)}, u32[]{:S(2)}, u32[]{:S(2)}) collective-permute-start(f32[64,512]{1,0:T(8,128)} %get-tuple-element.44), channel_id=1, source_target_pairs={{0,0},{1,2},{2,4},{3,6},{4,8},{5,10},{6,12},{7,14},{8,16},{9,18},{... | collective-permute-start | bytes 393224 | tf_op jit(solution)/shard_map/ppermute | solution.py:59
  350.2 5.7 %collective-permute-start.2 = (f32[64,512]{1,0:T(8,128)}, f32[64,512]{1,0:T(8,128)}, u32[]{:S(2)}, u32[]{:S(2)}) collective-permute-start(f32[64,512]{1,0:T(8,128)} %get-tuple-element.45), channel_id=1, source_target_pairs={{0,1},{1,3},{2,5},{3,7},{4,9},{5,11},{6,13},{7,15},{8,17},{9,19},{... | collective-permute-start | bytes 393224 | tf_op jit(solution)/shard_map/ppermute | solution.py:59
  360.2 129.3 %all-to-all-start = ((f32[64,64,512]{2,1,0:T(8,128)}), f32[64,64,512]{2,1,0:T(8,128)}, u32[]{:S(2)}, u32[]{:S(2)}) async-start(f32[64,64,512]{2,1,0:T(8,128)} %stack.2), calls=%async_computation | async-start | bytes 16777216 | tf_op jit(solution)/shard_map/all_to_all | solution.py:65
Sparse Core Ops, SparseCore 0:
  35.5 130.7 all-reduce.4
